TPU v7x, 32 devices: a whole 2x2x4 slice. The times are simulated.
32 devices in a mesh: ctx: 2 (over y), head: 4 (over x, core), video: 4 (over z).
Axes of the slice: x: 2, y: 2, z: 4, core: 2. Of those that a mesh axis runs over, the one named last changes fastest.
Arguments:
- attention_qkv: bfloat16 [3, 4, 256, 3072], P(None, 'video', 'ctx', 'head'), may hold values from -8 to 8
- inner_qkv: bfloat16 [3, 4, 256, 3072], P(None, 'video', 'ctx', 'head'), may hold values from -3 to 3
- learn_rate: float32 [4, 48, 256], P('video', 'head', 'ctx'), may hold values from 0.001 to 0.01
- segment_id: int32 [4, 256], P('video'), may hold values from 0 to 3, never falling along the last dimension, each value on 1 to 128 neighbouring positions
- video_length: int32 [4], P('video'), may hold values from 128 to 256, as said below
- gate_alpha: float32 [3072], P('head'), may hold values from -1.5 to 1.5
- inner_gain: float32 [48, 64], P('head'), may hold values from 0.5 to 1.5
- inner_shift: float32 [48, 64], P('head'), may hold values from -3 to 3
- first_weight: bfloat16 [48, 64, 256], P('head'), may hold values from -0.75 to 0.75
- first_bias: float32 [48, 256], P('head'), may hold values from -3 to 3
- second_weight: bfloat16 [48, 256, 64], P('head'), may hold values from -0.375 to 0.375
- second_bias: float32 [48, 64], P('head'), may hold values from -3 to 3
- out_weight: bfloat16 [3072, 3072], P('head', 'video'), may hold values from -0.109375 to 0.109375
Outputs:
- mixed: bfloat16 [4, 256, 3072], P('video', 'ctx', 'head')
Inputs may be any that keep to these rules, and one draw needn't show every extreme that they name: `segment_id`: segment numbers never fall along a video; each segment holds 1 to 128 positions and some segment exactly 128. `video_length`: some video is live in all 256 positions.
All inputs are finite; a program needn't handle non-finite values.
Results may differ from a plain program's by a relative error of at most 0.017.
Values may be sent and summed in bfloat16 or wider, within the bound.
A program may use at most 64 MiB of HBM per device.

v0:
```python
from functools import partial

import jax
import jax.numpy as jnp
from jax import lax
from jax.sharding import PartitionSpec as P

HD = 64
MB = 64


gelu_scale = 0.7978845608028654
gelu_cubic = 0.044715


def with_halo(cells, sides, width):
    for axis, dim in sides:
        count = lax.axis_size(axis)
        ends = count - 1
        head = lax.slice_in_dim(cells, 0, width, axis=dim)
        tail = lax.slice_in_dim(cells, cells.shape[dim] - width, cells.shape[dim], axis=dim)
        cells = jnp.concatenate(
            [
                lax.ppermute(tail, axis, [(i, (i + 1) % count) for i in range(ends)]),
                cells,
                lax.ppermute(head, axis, [((i + 1) % count, i) for i in range(ends)]),
            ],
            axis=dim,
        )
    return cells


def matmul_high(first_op, second_op):
    return jnp.matmul(first_op, second_op, precision=lax.Precision.HIGHEST)


def gelu_pair(entries):
    inner_arg = gelu_scale * (entries + gelu_cubic * entries * entries * entries)
    tanh_val = jnp.tanh(inner_arg)
    act_val = 0.5 * entries * (1.0 + tanh_val)
    slope_val = 0.5 * (1.0 + tanh_val) + 0.5 * entries * (
        1.0 - tanh_val * tanh_val
    ) * gelu_scale * (1.0 + 3.0 * gelu_cubic * entries * entries)
    return (act_val, slope_val)


def layer_stats(summed):
    center = summed - jnp.mean(summed, axis=-1, keepdims=True)
    variance = jnp.mean(center * center, axis=-1, keepdims=True)
    inv_std = lax.rsqrt(variance + 1e-06)
    return (center * inv_std, inv_std)


def lower_mask(row_count):
    row_ids = lax.broadcasted_iota(jnp.int32, (row_count, row_count), 0)
    col_ids = lax.broadcasted_iota(jnp.int32, (row_count, row_count), 1)
    return (row_ids >= col_ids).astype(jnp.float32)


def inner_update(inner_state, key_mb, value_mb, rate_mb, norm_gain, norm_shift):
    weight_one, bias_one, weight_two, bias_two = inner_state
    hidden_pre = matmul_high(key_mb, weight_one) + bias_one
    hidden_act, hidden_slope = gelu_pair(hidden_pre)
    output_pre = matmul_high(hidden_act, weight_two) + bias_two
    normed, inv_std = layer_stats(output_pre)
    residual_err = norm_gain * normed + norm_shift - (value_mb - key_mb)
    scaled_err = residual_err * norm_gain
    grad_two = inv_std * (
        scaled_err
        - jnp.mean(scaled_err, axis=-1, keepdims=True)
        - normed * jnp.mean(scaled_err * normed, axis=-1, keepdims=True)
    )
    grad_one = matmul_high(grad_two, weight_two.T) * hidden_slope
    grad_one = grad_one * rate_mb[:, None]
    grad_two = grad_two * rate_mb[:, None]
    new_state = (
        weight_one - matmul_high(key_mb.T, grad_one),
        bias_one - jnp.sum(grad_one, axis=0),
        weight_two - matmul_high(hidden_act.T, grad_two),
        bias_two - jnp.sum(grad_two, axis=0),
    )
    return ((grad_one, hidden_act, grad_two), new_state)


def query_side(inner_state, query_mb, key_mb, grad_pack, norm_gain, norm_shift):
    weight_one, bias_one, weight_two, bias_two = inner_state
    grad_one, hidden_act, grad_two = grad_pack
    causal = lower_mask(query_mb.shape[0])
    first_kernel = (matmul_high(query_mb, key_mb.T) + 1.0) * causal
    query_pre = matmul_high(query_mb, weight_one) + bias_one - matmul_high(first_kernel, grad_one)
    query_act, unused_slope = gelu_pair(query_pre)
    second_kernel = (matmul_high(query_act, hidden_act.T) + 1.0) * causal
    query_out = matmul_high(query_act, weight_two) + bias_two - matmul_high(second_kernel, grad_two)
    normed, unused_inv = layer_stats(query_out)
    return query_mb + norm_gain * normed + norm_shift


def chain_scan(
    keep_queries, inner_state, queries, key_rows, values, rate_vals, norm_gain, norm_shift
):

    def stepper(loop_state, inputs):
        query_mb, key_mb, value_mb, rate_mb = inputs
        grad_pack, new_state = inner_update(
            loop_state, key_mb, value_mb, rate_mb, norm_gain, norm_shift
        )
        return (
            new_state,
            query_side(loop_state, query_mb, key_mb, grad_pack, norm_gain, norm_shift),
        )

    return lax.scan(stepper, inner_state, (queries, key_rows, values, rate_vals))


def pad_heads(array_in, total_heads, fill_value):
    extra = total_heads - array_in.shape[0]
    filler = jnp.full((extra,) + array_in.shape[1:], fill_value, array_in.dtype)
    return jnp.concatenate([array_in, filler], axis=0)


def on_device(
    attention_qkv,
    inner_qkv,
    learn_rate,
    segment_id,
    video_length,
    gate_alpha,
    inner_gain,
    inner_shift,
    first_weight,
    first_bias,
    second_weight,
    second_bias,
    out_weight,
):
    tok_count = attention_qkv.shape[2]
    width_dev = attention_qkv.shape[3]
    heads_dev = width_dev // HD
    ctx_index = lax.axis_index("ctx")
    ctx_count = lax.axis_size("ctx")
    positions = ctx_index * tok_count + jnp.arange(tok_count, dtype=jnp.int32)
    length_val = video_length[0]
    live_rows = (positions < length_val).astype(jnp.float32)
    kv_pair = attention_qkv[1:, 0]
    kv_wide = with_halo(kv_pair, (("ctx", 1),), tok_count)
    key_pos = (ctx_index - 1) * tok_count + jnp.arange(3 * tok_count, dtype=jnp.int32)
    seg_row = segment_id[0]
    fill_ids = jnp.full((tok_count,), -1, jnp.int32)
    seg_pad = jnp.concatenate([fill_ids, seg_row, fill_ids])
    key_seg = lax.dynamic_slice_in_dim(seg_pad, ctx_index * tok_count, 3 * tok_count, 0)
    query_seg = lax.dynamic_slice_in_dim(seg_row, ctx_index * tok_count, tok_count, 0)
    allowed = (key_seg[None, :] == query_seg[:, None]) & (
        (key_pos[None, :] < length_val) | (key_pos[None, :] == positions[:, None])
    )
    query_heads = attention_qkv[0, 0].reshape(tok_count, heads_dev, HD)
    key_heads = kv_wide[0].reshape(3 * tok_count, heads_dev, HD)
    value_heads = kv_wide[1].reshape(3 * tok_count, heads_dev, HD)
    scores = jnp.einsum(
        "qhd,khd->hqk", query_heads, key_heads, preferred_element_type=jnp.float32
    ) * HD ** (-0.5)
    scores = jnp.where(allowed[None], scores, -1e30)
    row_max = jnp.max(scores, axis=-1, keepdims=True)
    exp_scores = jnp.exp(scores - row_max)
    soft_weights = (exp_scores / jnp.sum(exp_scores, axis=-1, keepdims=True)).astype(jnp.bfloat16)
    attended = jnp.einsum(
        "hqk,khd->qhd", soft_weights, value_heads, preferred_element_type=jnp.float32
    ).reshape(tok_count, width_dev)
    init_state = (
        first_weight.astype(jnp.float32),
        first_bias,
        second_weight.astype(jnp.float32),
        second_bias,
    )
    rate_rows = learn_rate[0] * live_rows[None, :]
    heads_each = -(-heads_dev // ctx_count)
    heads_padded = heads_each * ctx_count
    rows_heads = inner_qkv[:, 0].reshape(3, tok_count, heads_dev, HD)
    rows_padded = jnp.concatenate(
        [rows_heads, jnp.zeros((3, tok_count, heads_padded - heads_dev, HD), rows_heads.dtype)],
        axis=2,
    )
    rates_padded = pad_heads(rate_rows, heads_padded, 0.0)
    whole_rows = lax.all_to_all(rows_padded, "ctx", split_axis=2, concat_axis=1, tiled=True)
    whole_rates = lax.all_to_all(rates_padded, "ctx", split_axis=0, concat_axis=1, tiled=True)
    seq_count = whole_rows.shape[1]
    full_batches = seq_count // MB
    local_qkv = (
        whole_rows.astype(jnp.float32)
        .transpose(0, 2, 1, 3)
        .reshape(3, heads_each, full_batches, MB, HD)
    )
    local_rates = whole_rates.reshape(heads_each, full_batches, MB)
    first_head = ctx_index * heads_each
    local_gain = lax.dynamic_slice_in_dim(
        pad_heads(inner_gain, heads_padded, 1.0), first_head, heads_each, 0
    )
    local_shift = lax.dynamic_slice_in_dim(
        pad_heads(inner_shift, heads_padded, 0.0), first_head, heads_each, 0
    )
    local_state = tuple(
        (
            lax.dynamic_slice_in_dim(
                pad_heads(piece_arr, heads_padded, 0.0), first_head, heads_each, 0
            )
            for piece_arr in init_state
        )
    )
    unused_final, saved_local = jax.vmap(partial(chain_scan, True))(
        local_state, local_qkv[0], local_qkv[1], local_qkv[2], local_rates, local_gain, local_shift
    )
    out_rows = saved_local.reshape(heads_each, seq_count, HD).transpose(1, 0, 2)
    back_rows = lax.all_to_all(
        out_rows.astype(jnp.bfloat16), "ctx", split_axis=0, concat_axis=1, tiled=True
    ).astype(out_rows.dtype)
    inner_flat = back_rows[:, :heads_dev].reshape(tok_count, width_dev)
    combined = ((attended + jnp.tanh(gate_alpha) * inner_flat) * live_rows[:, None]).astype(
        jnp.bfloat16
    )
    terms = jnp.dot(
        combined,
        lax.all_gather(out_weight, "video", axis=1, tiled=True),
        preferred_element_type=jnp.float32,
    )
    mixed = lax.psum_scatter(terms.astype(jnp.bfloat16), "head", scatter_dimension=1, tiled=True)
    return mixed[None]


def solution(mesh):
    placed = (
        P(None, "video", "ctx", "head"),
        P(None, "video", "ctx", "head"),
        P("video", "head", "ctx"),
        P("video", None),
        P("video"),
        P("head"),
        P("head", None),
        P("head", None),
        P("head", None, None),
        P("head", None),
        P("head", None, None),
        P("head", None),
        P("head", "video"),
    )
    return jax.shard_map(
        on_device, mesh=mesh, in_specs=placed, out_specs=P("video", "ctx", "head"), check_vma=False
    )
```

profile of v0, /device:TPU:1, one launch (start us, length us, event | category | flops | bytes accessed | tf_op | source)
XLA Modules:
  0.0 147.5 jit_solution(2248685668227218046)
XLA Ops:
  6.6 1.9 %slice_bitcast_fusion = bf16[2,128,768]{2,1,0:T(8,128)(2,1)} fusion(bf16[3,1,128,768]{3,2,1,0:T(8,128)(2,1)} %param.15), kind=kLoop, calls=%fused_computation.74 | loop fusion | bytes 786432 | tf_op jit(solution)/shard_map/squeeze | solution.py:144
  8.5 4.7 %collective-permute-start = (bf16[2,128,768]{2,1,0:T(8,128)(2,1)}, bf16[2,128,768]{2,1,0:T(8,128)(2,1)}, u32[]{:S(2)}, u32[]{:S(2)}) collective-permute-start(bf16[2,128,768]{2,1,0:T(8,128)(2,1)} %slice_bitcast_fusion), channel_id=1, source_target_pairs={{0,16},{1,17},{2,18},{3,19},{4,20},{5,21},{6,22},{7,23},{8,24},{9,... | collective-permute-start | bytes 1179656 | tf_op jit(solution)/shard_map/ppermute | solution.py:24
  13.2 1.3 collective-permute-start.1
  15.1 0.7 reduce
  16.5 4.1 %all-to-all-start.1 = ((f32[2,6,128]{2,1,0:T(8,128)}), f32[2,6,128]{2,1,0:T(8,128)S(1)}, u32[]{:S(2)}, u32[]{:S(2)}) async-start(f32[2,6,128]{2,1,0:T(8,128)} %broadcast_multiply_fusion.4), calls=%async_computation.1 | async-start | bytes 16384 | tf_op jit(solution)/shard_map/all_to_all | solution.py:184
  20.6 0.7 all-gather.2.cloned.1.call-update
  21.3 1.0 dynamic-slice_convert_fusion
  22.5 0.8 copy.92
  23.6 0.9 copy.95
  25.2 3.5 %all-to-all-start = ((bf16[3,128,12,64]{1,3,0,2:T(8,128)(2,1)}), bf16[3,128,12,64]{1,3,0,2:T(8,128)(2,1)S(1)}, u32[]{:S(2)}, u32[]{:S(2)}) async-start(bf16[3,128,12,64]{1,3,0,2:T(8,128)(2,1)} %copy.95), calls=%async_computation | async-start | bytes 1179648 | tf_op jit(solution)/shard_map/all_to_all | solution.py:183
  29.0 6.7 %all-to-all-done = bf16[3,128,12,64]{1,3,0,2:T(8,128)(2,1)S(1)} async-done(((bf16[3,128,12,64]{1,3,0,2:T(8,128)(2,1)}), bf16[3,128,12,64]{1,3,0,2:T(8,128)(2,1)S(1)}, u32[]{:S(2)}, u32[]{:S(2)}) %all-to-all-start) | async-done | bytes 589856 | tf_op jit(solution)/shard_map/all_to_all | solution.py:183
  36.3 1.2 squeeze.37
  37.5 1.3 squeeze.39
  38.8 44.1 %while.18 = (s32[]{:T(128)}, f32[6,64,256]{2,1,0:T(8,128)S(1)}, f32[6,256]{1,0:T(8,128)S(1)}, f32[6,256,64]{1,2,0:T(8,128)S(1)}, f32[6,64]{1,0:T(8,128)S(1)}, /*...) while((s32[]{:T(128)}, f32[6,64,256]{2,1,0:T(8,128)S(1)}, ...), condition=%wide.region_11.12_spmd, body=%wide.region_2.11_spmd.sunk | while | flops 723821312 | bytes 12838537 | solution.py:112
  39.6 0.7 fusion.114
  40.5 1.8 %constant_dynamic-slice_fusion.14 = (f32[1,6,64,64]{2,0,3,1:T(1,128)S(1)}, f32[1,6,64,64]{2,0,3,1:T(1,128)S(1)}) fusion(f32[4,6,64,64]{2,0,3,1:T(4,128)} %get-tuple-element.296, s32[]{:T(128)} %get-tuple-element.272, f32[4,6,64,64]{2,0,3,1:T(4,128)} %get-tuple-element.294), kind=kLoop, calls=%fused_computation.52.clone.1 | loop fusion | bytes 393220 | tf_op jit(solution)/shard_map/vmap()/while/body/jit(dynamic_index_in_dim)/dynamic_slice | solution.py:112
  43.3 0.7 fusion.116
  45.6 0.6 fusion.120
  47.7 0.8 bitcast_dynamic-update-slice_fusion.2
  48.5 0.8 convolution_subtract_fusion.7
  50.6 0.7 fusion.114
  51.6 1.8 %constant_dynamic-slice_fusion.14 = (f32[1,6,64,64]{2,0,3,1:T(1,128)S(1)}, f32[1,6,64,64]{2,0,3,1:T(1,128)S(1)}) fusion(f32[4,6,64,64]{2,0,3,1:T(4,128)} %get-tuple-element.296, s32[]{:T(128)} %get-tuple-element.272, f32[4,6,64,64]{2,0,3,1:T(4,128)} %get-tuple-element.294), kind=kLoop, calls=%fused_computation.52.clone.1 | loop fusion | bytes 393220 | tf_op jit(solution)/shard_map/vmap()/while/body/jit(dynamic_index_in_dim)/dynamic_slice | solution.py:112
  54.4 0.7 fusion.116
  56.7 0.6 fusion.120
  58.7 0.8 bitcast_dynamic-update-slice_fusion.2
  59.5 0.8 convolution_subtract_fusion.7
  61.7 0.7 fusion.114
  62.6 1.8 %constant_dynamic-slice_fusion.14 = (f32[1,6,64,64]{2,0,3,1:T(1,128)S(1)}, f32[1,6,64,64]{2,0,3,1:T(1,128)S(1)}) fusion(f32[4,6,64,64]{2,0,3,1:T(4,128)} %get-tuple-element.296, s32[]{:T(128)} %get-tuple-element.272, f32[4,6,64,64]{2,0,3,1:T(4,128)} %get-tuple-element.294), kind=kLoop, calls=%fused_computation.52.clone.1 | loop fusion | bytes 393220 | tf_op jit(solution)/shard_map/vmap()/while/body/jit(dynamic_index_in_dim)/dynamic_slice | solution.py:112
  65.4 0.7 fusion.116
  67.7 0.6 fusion.120
  69.7 0.8 bitcast_dynamic-update-slice_fusion.2
  70.5 0.8 convolution_subtract_fusion.7
  72.7 0.7 fusion.114
  73.6 1.8 %constant_dynamic-slice_fusion.14 = (f32[1,6,64,64]{2,0,3,1:T(1,128)S(1)}, f32[1,6,64,64]{2,0,3,1:T(1,128)S(1)}) fusion(f32[4,6,64,64]{2,0,3,1:T(4,128)} %get-tuple-element.296, s32[]{:T(128)} %get-tuple-element.272, f32[4,6,64,64]{2,0,3,1:T(4,128)} %get-tuple-element.294), kind=kLoop, calls=%fused_computation.52.clone.1 | loop fusion | bytes 393220 | tf_op jit(solution)/shard_map/vmap()/while/body/jit(dynamic_index_in_dim)/dynamic_slice | solution.py:112
  76.4 0.7 fusion.116
  78.7 0.6 fusion.120
  80.8 0.8 bitcast_dynamic-update-slice_fusion.2
  81.6 0.8 convolution_subtract_fusion.7
  82.9 1.2 copy.103
  84.8 1.0 reshape.187
  85.8 3.4 %all-to-all-start.2 = ((bf16[2,2,24576]{2,1,0:T(2,128)(2,1)}), bf16[2,2,24576]{2,1,0:T(2,128)(2,1)S(1)}, u32[]{:S(2)}, u32[]{:S(2)}) async-start(bf16[2,2,24576]{2,1,0:T(2,128)(2,1)} %reshape.187), calls=%async_computation.2 | async-start | bytes 393216 | tf_op jit(solution)/shard_map/all_to_all | solution.py:212
  89.5 1.3 pad_maximum_fusion
  91.6 1.8 %all-to-all-done.2 = bf16[2,2,24576]{2,1,0:T(2,128)(2,1)S(1)} async-done(((bf16[2,2,24576]{2,1,0:T(2,128)(2,1)}), bf16[2,2,24576]{2,1,0:T(2,128)(2,1)S(1)}, u32[]{:S(2)}, u32[]{:S(2)}) %all-to-all-start.2) | async-done | bytes 196640 | tf_op jit(solution)/shard_map/all_to_all | solution.py:212
  94.2 1.0 fusion.45
  95.2 1.2 fusion.24
  96.6 18.3 %all-gather.2.cloned.1.call-done = bf16[768,3072]{1,0:T(8,128)(2,1)} async-done(((bf16[768,768]{1,0:T(8,128)(2,1)}), bf16[768,3072]{1,0:T(8,128)(2,1)}) %all-gather.2.cloned.1.call-update) | async-done | bytes 4718608 | tf_op jit(solution)/shard_map/all_gather | solution.py:221
  114.9 4.0 %convolution_convert_fusion = bf16[128,3072]{1,0:T(8,128)(2,1)} fusion(bf16[128,768]{0,1:T(8,128)(2,1)S(1)} %fusion.27, bf16[768,3072]{1,0:T(8,128)(2,1)} %all-gather.2.cloned.1.call-done), kind=kOutput, calls=%fused_computation.57 | convolution fusion | flops 604372992 | bytes 5701632 | tf_op jit(solution)/shard_map/dot_general | solution.py:219
  118.9 21.7 %reduce-scatter.2.cloned.1.call-done = bf16[128,768]{1,0:T(8,128)(2,1)} async-done(((bf16[128,3072]{1,0:T(8,128)(2,1)}), bf16[128,768]{1,0:T(8,128)(2,1)}) %reduce-scatter.2.cloned.1.call-update) | async-done | bytes 196624 | tf_op jit(solution)/shard_map/reduce_scatter | solution.py:224
  (164 shorter events, 26.9 us)
Async XLA Ops:
  6.5 15.8 %copy-start = (f32[12,256]{1,0:T(8,128)S(1)}, f32[12,256]{1,0:T(8,128)}, u32[]{:S(2)}) copy-start(f32[12,256]{1,0:T(8,128)} %param.24) | copy-start | bytes 36868
  6.5 16.0 %slice-start = ((bf16[3,1,128,768]{3,2,1,0:T(8,128)(2,1)}), bf16[1,1,128,768]{3,2,1,0:T(8,128)(2,1)S(1)}, s32[]{:S(2)}) async-start(bf16[3,1,128,768]{3,2,1,0:T(8,128)(2,1)} %param.15), calls=%async_computation.6 | async-start | bytes 393216 | tf_op jit(solution)/shard_map/slice | solution.py:155
  6.5 15.7 %copy-start.3 = (bf16[12,64,256]{2,1,0:T(8,128)(2,1)S(1)}, bf16[12,64,256]{2,1,0:T(8,128)(2,1)}, u32[]{:S(2)}) copy-start(bf16[12,64,256]{2,1,0:T(8,128)(2,1)} %param.23) | copy-start | bytes 1179652
  6.5 15.8 %copy-start.5 = (f32[12,64]{1,0:T(8,128)S(1)}, f32[12,64]{1,0:T(8,128)}, u32[]{:S(2)}) copy-start(f32[12,64]{1,0:T(8,128)} %param.26) | copy-start | bytes 9220
  6.5 15.9 %copy-start.8 = (s32[1,256]{1,0:T(1,128)S(1)}, s32[1,256]{1,0:T(1,128)}, u32[]{:S(2)}) copy-start(s32[1,256]{1,0:T(1,128)} %param.18) | copy-start | bytes 3076
  6.5 15.9 %copy-start.7 = (f32[12,64]{1,0:T(8,128)S(1)}, f32[12,64]{1,0:T(8,128)}, u32[]{:S(2)}) copy-start(f32[12,64]{1,0:T(8,128)} %param.21) | copy-start | bytes 9220
  6.6 15.9 %copy-start.6 = (f32[12,64]{1,0:T(8,128)S(1)}, f32[12,64]{1,0:T(8,128)}, u32[]{:S(2)}) copy-start(f32[12,64]{1,0:T(8,128)} %param.22) | copy-start | bytes 9220
  6.6 16.8 %copy-start.1 = (bf16[3,1,128,768]{3,2,1,0:T(8,128)(2,1)S(1)}, bf16[3,1,128,768]{3,2,1,0:T(8,128)(2,1)}, u32[]{:S(2)}) copy-start(bf16[3,1,128,768]{3,2,1,0:T(8,128)(2,1)} %param.16) | copy-start | bytes 1769476
  8.5 81.0 %collective-permute-start = (bf16[2,128,768]{2,1,0:T(8,128)(2,1)}, bf16[2,128,768]{2,1,0:T(8,128)(2,1)}, u32[]{:S(2)}, u32[]{:S(2)}) collective-permute-start(bf16[2,128,768]{2,1,0:T(8,128)(2,1)} %slice_bitcast_fusion), channel_id=1, source_target_pairs={{0,16},{1,17},{2,18},{3,19},{4,20},{5,21},{6,22},{7,23},{8,24},{9,... | collective-permute-start | bytes 1179656 | tf_op jit(solution)/shard_map/ppermute | solution.py:24
  13.2 76.3 %collective-permute-start.1 = (bf16[2,128,768]{2,1,0:T(8,128)(2,1)}, bf16[2,128,768]{2,1,0:T(8,128)(2,1)}, u32[]{:S(2)}, u32[]{:S(2)}) collective-permute-start(bf16[2,128,768]{2,1,0:T(8,128)(2,1)} %slice_bitcast_fusion), channel_id=1, source_target_pairs={{16,0},{17,1},{18,2},{19,3},{20,4},{21,5},{22,6},{23,7},{24,8},{25... | collective-permute-start | bytes 1179656 | tf_op jit(solution)/shard_map/ppermute | solution.py:26
  16.5 8.7 %all-to-all-start.1 = ((f32[2,6,128]{2,1,0:T(8,128)}), f32[2,6,128]{2,1,0:T(8,128)S(1)}, u32[]{:S(2)}, u32[]{:S(2)}) async-start(f32[2,6,128]{2,1,0:T(8,128)} %broadcast_multiply_fusion.4), calls=%async_computation.1 | async-start | bytes 16384 | tf_op jit(solution)/shard_map/all_to_all | solution.py:184
  20.6 94.3 %all-gather.2.cloned.1.call-start = ((), (), s32[]{:S(2)}) async-start(), calls=%async_computation.4 | async-start | bytes 5898240 | tf_op jit(solution)/shard_map/all_gather | solution.py:221
  21.3 3.2 %copy-start.4 = (f32[768]{0:T(1024)S(1)}, f32[768]{0:T(1024)}, u32[]{:S(2)}) copy-start(f32[768]{0:T(1024)} %param.20) | copy-start | bytes 9220
  25.2 10.5 %all-to-all-start = ((bf16[3,128,12,64]{1,3,0,2:T(8,128)(2,1)}), bf16[3,128,12,64]{1,3,0,2:T(8,128)(2,1)S(1)}, u32[]{:S(2)}, u32[]{:S(2)}) async-start(bf16[3,128,12,64]{1,3,0,2:T(8,128)(2,1)} %copy.95), calls=%async_computation | async-start | bytes 1179648 | tf_op jit(solution)/shard_map/all_to_all | solution.py:183
  85.8 7.5 %all-to-all-start.2 = ((bf16[2,2,24576]{2,1,0:T(2,128)(2,1)}), bf16[2,2,24576]{2,1,0:T(2,128)(2,1)S(1)}, u32[]{:S(2)}, u32[]{:S(2)}) async-start(bf16[2,2,24576]{2,1,0:T(2,128)(2,1)} %reshape.187), calls=%async_computation.2 | async-start | bytes 393216 | tf_op jit(solution)/shard_map/all_to_all | solution.py:212
  89.3 51.4 %reduce-scatter.2.cloned.1.call-start = ((), (), s32[]{:S(2)}) async-start(), calls=%async_computation.5 | async-start | bytes 983040 | tf_op jit(solution)/shard_map/reduce_scatter | solution.py:224
  90.9 3.2 %copy-start.2 = (bf16[1,1,128,768]{2,3,1,0:T(8,128)(2,1)S(1)}, bf16[1,1,128,768]{2,3,1,0:T(8,128)(2,1)}, u32[]{:S(2)}) copy-start(bf16[1,1,128,768]{2,3,1,0:T(8,128)(2,1)} %copy.92) | copy-start | bytes 589828
Sparse Core Ops, SparseCore 0:
  22.9 91.9 all-gather.1
  119.1 21.5 reduce-scatter.1
where the time goes:
time: 149 us; the launch traced here: 147 us
  waiting for transfers between devices  49.8 us (33%)
  matrix products  32 us (21%)
  local copies, waits for them, and re-layouts  20.9 us (14%)
  starting transfers between devices  17.2 us (12%)
  between operations  14.5 us (10%)
  other arithmetic  12.1 us (8%)
    dot_general x44, matrix products, matmul_high(): return jnp.matmul(first_op, second_op, precision=lax.Precision.HIGHEST)  25.8 us
    reduce_scatter x1, waiting for transfers between devices, on_device(): lax.psum_scatter(terms.astype(jnp.bfloat16), 'head', scatter_dimension=1,...  21.7 us
    all_gather x1, waiting for transfers between devices, on_device(): lax.all_gather(out_weight, 'video', axis=1, tiled=True)  18.3 us
    dynamic_slice x28, local copies, waits for them, and re-layouts, chain_scan(): lax.scan(stepper, inner_state, (queries, key_rows, values, rate_vals))  9.39 us
    all_to_all x1, waiting for transfers between devices, on_device(): lax.all_to_all(rows_padded, 'ctx', split_axis=2, concat_axis=1, tiled=True)  6.66 us
    ppermute x1, starting transfers between devices, with_halo(): lax.ppermute(tail, axis, [(i, (i + 1) % count) for i in range(ends)])  4.71 us
    all_to_all x1, starting transfers between devices, on_device(): lax.all_to_all(rates_padded, 'ctx', split_axis=0, concat_axis=1, tiled=True)  4.1 us
    dot_general x1, matrix products, on_device(): jnp.dot(combined, lax.all_gather(out_weight, 'video', axis=1, tiled=True)...  4.04 us
  transfers between devices with their start and end apart: 7, of which 5 were waited for; matrix products, arithmetic and copies ran while one was open for 40% of the time, Pallas kernels for 0%

commit v1 on v0

--- a/solution.py
+++ b/solution.py
@@ -3,6 +3,8 @@
 import jax
 import jax.numpy as jnp
 from jax import lax
+from jax.experimental import pallas as pl
+from jax.experimental.pallas import tpu as pltpu
 from jax.sharding import PartitionSpec as P
 
 HD = 64
@@ -118,7 +120,564 @@
     return jnp.concatenate([array_in, filler], axis=0)
 
 
-def on_device(
+LANE = 128
+MESH_ID = pl.DeviceIdType.MESH
+
+
+def dot_nn(left, right):
+    return lax.dot_general(
+        left, right, (((1,), (0,)), ((), ())), preferred_element_type=jnp.float32
+    )
+
+
+def dot_nt(left, right):
+    return lax.dot_general(
+        left, right, (((1,), (1,)), ((), ())), preferred_element_type=jnp.float32
+    )
+
+
+def dot_tn(left, right):
+    return lax.dot_general(
+        left, right, (((0,), (0,)), ((), ())), preferred_element_type=jnp.float32
+    )
+
+
+def gelu_only(entries):
+    inner_arg = gelu_scale * (entries + gelu_cubic * entries * entries * entries)
+    return 0.5 * entries * (1.0 + jnp.tanh(inner_arg))
+
+
+def half_mean(cells, left):
+    first = jnp.sum(jnp.where(left, cells, 0.0), axis=-1, keepdims=True)
+    second = jnp.sum(jnp.where(left, 0.0, cells), axis=-1, keepdims=True)
+    return jnp.where(left, first, second) * (1.0 / HD)
+
+
+def half_stats(summed, left):
+    center = summed - half_mean(summed, left)
+    inv_std = lax.rsqrt(half_mean(center * center, left) + 1e-06)
+    return (center * inv_std, inv_std)
+
+
+def split_heads(cells, left):
+    wide = cells.astype(jnp.float32)
+    return jnp.concatenate(
+        [jnp.where(left, wide, 0.0), jnp.where(left, 0.0, wide)], axis=0
+    ).astype(cells.dtype)
+
+
+def fused_kernel(
+    aqkv,
+    iqkv,
+    rate,
+    first_w,
+    second_w,
+    out_w,
+    seg,
+    length,
+    gate,
+    gain,
+    shift,
+    first_b,
+    second_b,
+    out,
+    a_rows,
+    i_rows,
+    rates,
+    fw,
+    sw,
+    ow,
+    w1m,
+    w1b,
+    w2m,
+    w2b,
+    b1,
+    b2,
+    gain_s,
+    shift_s,
+    rate_a,
+    rate_b,
+    bias,
+    inner,
+    comb,
+    gathered,
+    parts,
+    arrived,
+    total,
+    load_sem,
+    y_send,
+    y_recv,
+    back_send,
+    back_recv,
+    z_send,
+    z_recv,
+    own_sem,
+    r_send,
+    r_recv,
+    t_send,
+    t_recv,
+):
+    slabs, _, seq, _ = a_rows.shape
+    tok = aqkv.shape[2]
+    hidden = first_b.shape[1]
+    count = lax.axis_size("head")
+    c = lax.axis_index("ctx")
+    h = lax.axis_index("head")
+    v = lax.axis_index("video")
+    other = 1 - c
+    mine = pl.multiple_of(c * tok, tok)
+    theirs = pl.multiple_of(other * tok, tok)
+    pairs_heads = 2 * slabs
+
+    def columns(owner, slab):
+        return pl.ds(pl.multiple_of((owner * slabs + slab) * LANE, LANE), LANE)
+
+    loads = []
+    for slab in range(slabs):
+        loads.append(
+            pltpu.make_async_copy(
+                iqkv.at[:, 0, :, columns(c, slab)],
+                i_rows.at[slab, :, pl.ds(mine, tok), :],
+                load_sem.at[slab],
+            )
+        )
+    loads.append(pltpu.make_async_copy(rate.at[0], rates.at[c], load_sem.at[2 * slabs]))
+    loads.append(
+        pltpu.make_async_copy(
+            first_w.at[pl.ds(c * pairs_heads, pairs_heads)], fw, load_sem.at[2 * slabs + 1]
+        )
+    )
+    loads.append(
+        pltpu.make_async_copy(
+            second_w.at[pl.ds(c * pairs_heads, pairs_heads)], sw, load_sem.at[2 * slabs + 2]
+        )
+    )
+    a_loads = [
+        pltpu.make_async_copy(
+            aqkv.at[:, 0, :, columns(c, slab)],
+            a_rows.at[slab, :, pl.ds(mine, tok), :],
+            load_sem.at[slabs + slab],
+        )
+        for slab in range(slabs)
+    ]
+    ow_load = pltpu.make_async_copy(out_w, ow, load_sem.at[2 * slabs + 3])
+    for copy in loads + a_loads + [ow_load]:
+        copy.start()
+
+    barrier = pltpu.get_barrier_semaphore()
+    pl.semaphore_signal(
+        barrier, inc=1, device_id={"ctx": other}, device_id_type=MESH_ID
+    )
+    everyone = count * count
+    place = h * count + v
+    for step in range(1, everyone):
+        peer = lax.rem(place + step, everyone)
+        pl.semaphore_signal(
+            barrier,
+            inc=1,
+            device_id={"head": peer // count, "video": lax.rem(peer, count)},
+            device_id_type=MESH_ID,
+        )
+    pl.semaphore_wait(barrier, everyone)
+
+    def to_partner(src, dst, send, recv):
+        return pltpu.make_async_remote_copy(
+            src_ref=src,
+            dst_ref=dst,
+            send_sem=send,
+            recv_sem=recv,
+            device_id={"ctx": other},
+            device_id_type=MESH_ID,
+        )
+
+    rate_out = to_partner(
+        rate.at[0], rates.at[c], y_send.at[2 * slabs], y_recv.at[2 * slabs]
+    )
+    rate_out.start()
+    i_out = [
+        to_partner(
+            iqkv.at[:, 0, :, columns(other, slab)],
+            i_rows.at[slab, :, pl.ds(mine, tok), :],
+            y_send.at[slab],
+            y_recv.at[slab],
+        )
+        for slab in range(slabs)
+    ]
+    a_out = [
+        to_partner(
+            aqkv.at[:, 0, :, columns(other, slab)],
+            a_rows.at[slab, :, pl.ds(mine, tok), :],
+            y_send.at[slabs + slab],
+            y_recv.at[slabs + slab],
+        )
+        for slab in range(slabs)
+    ]
+    for copy in i_out + a_out:
+        copy.start()
+
+    seq_ids = lax.broadcasted_iota(jnp.int32, (seq, seq), 1)
+    row_ids = lax.broadcasted_iota(jnp.int32, (seq, seq), 0)
+    len_val = length[0]
+    segs = jnp.broadcast_to(seg[...].astype(jnp.float32), (seq, seq))
+    allowed = (segs == segs.T) & ((seq_ids < len_val) | (seq_ids == row_ids))
+    bias[...] = jnp.where(allowed, 0.0, -1e30)
+    live = (lax.broadcasted_iota(jnp.int32, (seq, LANE), 0) < len_val).astype(jnp.float32)
+    left_row = lax.broadcasted_iota(jnp.int32, (1, LANE), 1) < HD
+    left = lax.broadcasted_iota(jnp.int32, (MB, LANE), 1) < HD
+    left_hidden = lax.broadcasted_iota(jnp.int32, (hidden, LANE), 1) < HD
+    left_seq = lax.broadcasted_iota(jnp.int32, (seq, LANE), 1) < HD
+    tri = lax.broadcasted_iota(jnp.int32, (MB, MB), 0) >= lax.broadcasted_iota(
+        jnp.int32, (MB, MB), 1
+    )
+    tri = tri.astype(jnp.float32)
+    tri_pair = jnp.concatenate([tri, tri], axis=0)
+
+    for copy in loads:
+        copy.wait()
+
+    def pair_row(ref, head):
+        return jnp.concatenate([ref[pl.ds(head, 1), :], ref[pl.ds(head + 1, 1), :]], axis=1)
+
+    for slab in range(slabs):
+        head = c * pairs_heads + 2 * slab
+        gain_s[slab] = pair_row(gain, head)
+        shift_s[slab] = pair_row(shift, head)
+        b1[slab] = pair_row(first_b, head)
+        b2[slab] = pair_row(second_b, head)
+        w1_a = fw[2 * slab]
+        w1_b = fw[2 * slab + 1]
+        w1m[slab, 0:HD] = w1_a.astype(jnp.float32)
+        w1m[slab, HD:LANE] = w1_b.astype(jnp.float32)
+        w1b[slab] = jnp.zeros_like(w1b[slab])
+        w1b[slab, 0:HD, 0:hidden] = w1_a
+        w1b[slab, HD:LANE, hidden : 2 * hidden] = w1_b
+        w2 = jnp.concatenate(
+            [sw[2 * slab].astype(jnp.float32), sw[2 * slab + 1].astype(jnp.float32)], axis=1
+        )
+        w2m[slab] = w2
+        w2b[slab, 0:hidden] = jnp.where(left_hidden, w2, 0.0).astype(jnp.bfloat16)
+        w2b[slab, hidden : 2 * hidden] = jnp.where(left_hidden, 0.0, w2).astype(jnp.bfloat16)
+
+    rate_out.wait_recv()
+    for slab in range(slabs):
+        head = c * pairs_heads + 2 * slab
+        for part in range(seq // tok):
+            rows = slice(part * tok, (part + 1) * tok)
+            for ahead, store in ((0, rate_a), (1, rate_b)):
+                row = rates[part, pl.ds(head + ahead, 1), :]
+                store[slab, rows] = jnp.broadcast_to(row, (LANE, tok)).T * live[rows]
+
+    for copy in i_out:
+        copy.wait_recv()
+
+    def inner_step(slab, row):
+        rows = pl.ds(row, MB)
+        query, key, value = (i_rows[slab, kind, rows, :] for kind in range(3))
+        query_f = query.astype(jnp.float32)
+        key_f = key.astype(jnp.float32)
+        value_f = value.astype(jnp.float32)
+        norm_gain = gain_s[slab]
+        norm_shift = shift_s[slab]
+        weight_one = w1b[slab]
+        weight_two = w2b[slab]
+        bias_one = b1[slab]
+        bias_two = b2[slab]
+        pre = dot_nn(jnp.concatenate([key, query], axis=0), weight_one) + bias_one
+        hidden_act, slope = gelu_pair(pre[:MB])
+        hidden_b = hidden_act.astype(jnp.bfloat16)
+        normed, inv_std = half_stats(dot_nn(hidden_b, weight_two) + bias_two, left)
+        scaled = (norm_gain * normed + norm_shift - (value_f - key_f)) * norm_gain
+        grad_two = inv_std * (
+            scaled - half_mean(scaled, left) - normed * half_mean(scaled * normed, left)
+        )
+        e_a = rate_a[slab, rows, :]
+        e_b = rate_b[slab, rows, :]
+        wide = [e_a] * (hidden // LANE) + [e_b] * (hidden // LANE)
+        grad_one = dot_nt(grad_two.astype(jnp.bfloat16), weight_two) * slope
+        grad_one = grad_one * jnp.concatenate(wide, axis=1)
+        grad_two = grad_two * jnp.where(left, e_a, e_b)
+        one_b = grad_one.astype(jnp.bfloat16)
+        two_b = grad_two.astype(jnp.bfloat16)
+
+        first_kernel = (dot_nt(split_heads(query, left), key) + 1.0) * tri_pair
+        first_kernel = first_kernel.astype(jnp.bfloat16)
+        fix = jnp.concatenate(
+            [
+                dot_nn(first_kernel[:MB], one_b[:, :hidden]),
+                dot_nn(first_kernel[MB:], one_b[:, hidden:]),
+            ],
+            axis=1,
+        )
+        query_act = gelu_only(pre[MB:] - fix).astype(jnp.bfloat16)
+        second_kernel = jnp.concatenate(
+            [
+                dot_nt(query_act[:, :hidden], hidden_b[:, :hidden]),
+                dot_nt(query_act[:, hidden:], hidden_b[:, hidden:]),
+            ],
+            axis=0,
+        )
+        second_kernel = ((second_kernel + 1.0) * tri_pair).astype(jnp.bfloat16)
+        fix_two = dot_nn(second_kernel, two_b)
+        fix_two = jnp.where(left, fix_two[:MB], fix_two[MB:])
+        query_out = dot_nn(query_act, weight_two) + bias_two - fix_two
+        normed_out, _ = half_stats(query_out, left)
+        inner[slab, rows, :] = query_f + norm_gain * normed_out + norm_shift
+
+        up_one = dot_tn(key, one_b)
+        one_first = w1m[slab, 0:HD] - up_one[:HD, :hidden]
+        one_second = w1m[slab, HD:LANE] - up_one[HD:, hidden:]
+        up_two = dot_tn(hidden_b, two_b)
+        two_new = w2m[slab] - jnp.where(left_hidden, up_two[:hidden], up_two[hidden:])
+        w1m[slab, 0:HD] = one_first
+        w1m[slab, HD:LANE] = one_second
+        w1b[slab, 0:HD, 0:hidden] = one_first.astype(jnp.bfloat16)
+        w1b[slab, HD:LANE, hidden : 2 * hidden] = one_second.astype(jnp.bfloat16)
+        w2m[slab] = two_new
+        w2b[slab, 0:hidden] = jnp.where(left_hidden, two_new, 0.0).astype(jnp.bfloat16)
+        w2b[slab, hidden : 2 * hidden] = jnp.where(left_hidden, 0.0, two_new).astype(
+            jnp.bfloat16
+        )
+        b1[slab] = bias_one - jnp.sum(grad_one, axis=0, keepdims=True)
+        b2[slab] = bias_two - jnp.sum(grad_two, axis=0, keepdims=True)
+
+    def batch_step(batch, carry):
+        row = pl.multiple_of(batch * MB, MB)
+        for slab in range(slabs):
+            inner_step(slab, row)
+        return carry
+
+    lax.fori_loop(0, seq // MB, batch_step, 0)
+
+    def to_video(src, video, spot, step):
+        return pltpu.make_async_remote_copy(
+            src_ref=src,
+            dst_ref=gathered.at[v, spot],
+            send_sem=z_send.at[spot, step - 1],
+            recv_sem=z_recv.at[spot, step - 1],
+            device_id={"video": video},
+            device_id_type=MESH_ID,
+        )
+
+    def spread(src, spot):
+        copies = []
+        for step in range(1, count):
+            copy = to_video(src, lax.rem(v + step, count), spot, step)
+            copy.start()
+            copies.append(copy)
+        return copies
+
+    z_out = []
+    backs = []
+    owns = []
+    for slab in range(slabs):
+        a_loads[slab].wait()
+        a_out[slab].wait_recv()
+        query, key, value = (a_rows[slab, kind] for kind in range(3))
+        scores = dot_nt(split_heads(query, left_seq), key) * HD ** (-0.5)
+        halves = []
+        for part in range(2):
+            mine_scores = scores[part * seq : (part + 1) * seq] + bias[...]
+            top = jnp.max(mine_scores, axis=-1, keepdims=True)
+            weights = jnp.exp(mine_scores - top)
+            mass = jnp.sum(weights, axis=-1, keepdims=True)
+            halves.append(dot_nn(weights.astype(jnp.bfloat16), value) / mass)
+        attended = jnp.where(left_seq, halves[0], halves[1])
+        gate_row = jnp.tanh(gate[:, columns(c, slab)])
+        comb[slab] = ((attended + gate_row * inner[slab]) * live).astype(jnp.bfloat16)
+        spot = c * slabs + slab
+        back = to_partner(
+            comb.at[slab, pl.ds(theirs, tok), :],
+            gathered.at[v, spot],
+            back_send.at[slab],
+            back_recv.at[slab],
+        )
+        back.start()
+        backs.append(back)
+        own = pltpu.make_async_copy(
+            comb.at[slab, pl.ds(mine, tok), :], gathered.at[v, spot], own_sem.at[slab]
+        )
+        own.start()
+        owns.append(own)
+        z_out += spread(comb.at[slab, pl.ds(mine, tok), :], spot)
+        if slab:
+            backs[slab - 1].wait_recv()
+            far = other * slabs + slab - 1
+            z_out += spread(gathered.at[v, far], far)
+    backs[slabs - 1].wait_recv()
+    far = other * slabs + slabs - 1
+    z_out += spread(gathered.at[v, far], far)
+    for own in owns:
+        own.wait()
+    ow_load.wait()
+
+    def owner_of(video):
+        return lax.rem(video, 2) * (count // 2) + video // 2
+
+    def video_of(head):
+        return lax.rem(head, count // 2) * 2 + head // (count // 2)
+
+    for step in range(1, count):
+        source = lax.rem(v + count - step, count)
+        for spot in range(2 * slabs):
+            pltpu.make_async_remote_copy(
+                src_ref=gathered.at[source, spot],
+                dst_ref=gathered.at[source, spot],
+                send_sem=z_send.at[spot, step - 1],
+                recv_sem=z_recv.at[spot, step - 1],
+                device_id={"video": source},
+                device_id_type=MESH_ID,
+            ).wait_recv()
+    rows_all = jnp.concatenate(
+        [
+            jnp.concatenate([gathered[video, spot] for spot in range(2 * slabs)], axis=1)
+            for video in range(count)
+        ],
+        axis=0,
+    )
+    width = ow.shape[1]
+    chunk = 2 * LANE if width % (2 * LANE) == 0 else width
+    for start in range(0, width, chunk):
+        piece = dot_nn(rows_all, ow[:, start : start + chunk]).astype(jnp.bfloat16)
+        for video in range(count):
+            parts[video, :, start : start + chunk] = piece[video * tok : (video + 1) * tok]
+
+    r_out = []
+    for step in range(count - 1, 0, -1):
+        head = lax.rem(h + step, count)
+        copy = pltpu.make_async_remote_copy(
+            src_ref=parts.at[video_of(head)],
+            dst_ref=arrived.at[step - 1],
+            send_sem=r_send.at[step - 1],
+            recv_sem=r_recv.at[step - 1],
+            device_id={"head": head},
+            device_id_type=MESH_ID,
+        )
+        copy.start()
+        r_out.append(copy)
+    for copy in r_out:
+        copy.wait_recv()
+    summed = parts[video_of(h)].astype(jnp.float32)
+    for step in range(count - 1):
+        summed = summed + arrived[step].astype(jnp.float32)
+    total[...] = summed.astype(jnp.bfloat16)
+
+    to_head, to_v = v, video_of(h)
+    stays = (to_head == h) & (to_v == v)
+    final = pltpu.make_async_remote_copy(
+        src_ref=total,
+        dst_ref=out.at[0],
+        send_sem=t_send,
+        recv_sem=t_recv,
+        device_id={"head": to_head, "video": to_v},
+        device_id_type=MESH_ID,
+    )
+
+    @pl.when(stays)
+    def _():
+        out[0] = total[...]
+
+    @pl.when(jnp.logical_not(stays))
+    def _():
+        final.start()
+        final.wait()
+
+    for copy in [rate_out] + i_out + a_out + backs + z_out + r_out:
+        copy.wait_send()
+
+
+def fused_on_device(
+    attention_qkv,
+    inner_qkv,
+    learn_rate,
+    segment_id,
+    video_length,
+    gate_alpha,
+    inner_gain,
+    inner_shift,
+    first_weight,
+    first_bias,
+    second_weight,
+    second_bias,
+    out_weight,
+):
+    tok = attention_qkv.shape[2]
+    width_dev = attention_qkv.shape[3]
+    count = lax.axis_size("head")
+    ctx_count = lax.axis_size("ctx")
+    seq = tok * ctx_count
+    slabs = width_dev // LANE // ctx_count
+    heads = width_dev // HD
+    hidden = first_weight.shape[2]
+    columns = out_weight.shape[1]
+    half = jnp.bfloat16
+    full = jnp.float32
+    hbm = pl.BlockSpec(memory_space=pl.ANY)
+    vmem = pl.BlockSpec(memory_space=pltpu.VMEM)
+    smem = pl.BlockSpec(memory_space=pltpu.SMEM)
+    dma = pltpu.SemaphoreType.DMA
+    return pl.pallas_call(
+        fused_kernel,
+        out_shape=jax.ShapeDtypeStruct((1, tok, columns), half),
+        in_specs=[hbm] * 6 + [vmem, smem] + [vmem] * 5,
+        out_specs=vmem,
+        scratch_shapes=[
+            pltpu.VMEM((slabs, 3, seq, LANE), half),
+            pltpu.VMEM((slabs, 3, seq, LANE), half),
+            pltpu.VMEM((ctx_count, heads, tok), full),
+            pltpu.VMEM((2 * slabs,) + first_weight.shape[1:], half),
+            pltpu.VMEM((2 * slabs,) + second_weight.shape[1:], half),
+            pltpu.VMEM(out_weight.shape, half),
+            pltpu.VMEM((slabs, LANE, hidden), full),
+            pltpu.VMEM((slabs, LANE, 2 * hidden), half),
+            pltpu.VMEM((slabs, hidden, LANE), full),
+            pltpu.VMEM((slabs, 2 * hidden, LANE), half),
+            pltpu.VMEM((slabs, 1, 2 * hidden), full),
+            pltpu.VMEM((slabs, 1, LANE), full),
+            pltpu.VMEM((slabs, 1, LANE), full),
+            pltpu.VMEM((slabs, 1, LANE), full),
+            pltpu.VMEM((slabs, seq, LANE), full),
+            pltpu.VMEM((slabs, seq, LANE), full),
+            pltpu.VMEM((seq, seq), full),
+            pltpu.VMEM((slabs, seq, LANE), full),
+            pltpu.VMEM((slabs, seq, LANE), half),
+            pltpu.VMEM((count, 2 * slabs, tok, LANE), half),
+            pltpu.VMEM((count, tok, columns), half),
+            pltpu.VMEM((count - 1, tok, columns), half),
+            pltpu.VMEM((tok, columns), half),
+            dma((2 * slabs + 4,)),
+            dma((2 * slabs + 1,)),
+            dma((2 * slabs + 1,)),
+            dma((slabs,)),
+            dma((slabs,)),
+            dma((2 * slabs, count - 1)),
+            dma((2 * slabs, count - 1)),
+            dma((slabs,)),
+            dma((count - 1,)),
+            dma((count - 1,)),
+            dma,
+            dma,
+        ],
+        compiler_params=pltpu.CompilerParams(
+            collective_id=0, has_side_effects=True, vmem_limit_bytes=60 * 1024 * 1024
+        ),
+    )(
+        attention_qkv,
+        inner_qkv,
+        learn_rate,
+        first_weight,
+        second_weight,
+        out_weight,
+        segment_id,
+        video_length,
+        gate_alpha[None],
+        inner_gain,
+        inner_shift,
+        first_bias,
+        second_bias,
+    )
+
+
+def general_on_device(
     attention_qkv,
     inner_qkv,
     learn_rate,
@@ -241,6 +800,15 @@
         P("head", None),
         P("head", "video"),
     )
+    shape = mesh.shape
+    fused = shape["ctx"] == 2 and shape["head"] == shape["video"] and shape["head"] % 2 == 0
+
+    def on_device(*args):
+        heads_dev = args[0].shape[3] // HD
+        if fused and heads_dev % (2 * shape["ctx"]) == 0 and args[0].shape[2] % 128 == 0:
+            return fused_on_device(*args)
+        return general_on_device(*args)
+
     return jax.shard_map(
         on_device, mesh=mesh, in_specs=placed, out_specs=P("video", "ctx", "head"), check_vma=False
     )

time: 149 us -> 74.3 us (0.50)
  Pallas kernels: 0 us -> 67 us
  waiting for transfers between devices: 49.8 us -> 0 us
  matrix products: 32 us -> 0 us
  starting transfers between devices: 17.2 us -> 0 us
  local copies, waits for them, and re-layouts: 20.9 us -> 6.34 us
  between operations: 14.5 us -> 0.66 us
  other arithmetic: 12.1 us -> 0 us
    pallas_call x0 -> x1, Pallas kernels: none -> 67 us  [fused_on_device(): pl.pallas_call(fused_kernel, out_shape=jax.ShapeDtypeStruct((1, tok, colu...]
    dot_general x46 -> x0, matrix products: 31 us -> none  [the longest x44 25.8 us: matmul_high(): return jnp.matmul(first_op, second_op, precision=lax.Precision.HIGHEST)]
    reduce_scatter x1 -> x0, waiting for transfers between devices: 21.7 us -> none  [on_device(): lax.psum_scatter(terms.astype(jnp.bfloat16), 'head', scatter_dimension=1,...]
    all_gather x1 -> x0, waiting for transfers between devices: 18.3 us -> none  [on_device(): lax.all_gather(out_weight, 'video', axis=1, tiled=True)]
    all_to_all x3 -> x0, starting transfers between devices: 11 us -> none  [the longest x1 4.1 us: on_device(): lax.all_to_all(rates_padded, 'ctx', split_axis=0, concat_axis=1, tiled=True)]
    dynamic_slice x32 -> x0, local copies, waits for them, and re-layouts: 9.51 us -> none  [the longest x28 9.39 us: chain_scan(): lax.scan(stepper, inner_state, (queries, key_rows, values, rate_vals))]
    all_to_all x3 -> x0, waiting for transfers between devices: 9.01 us -> none  [the longest x1 6.66 us: on_device(): lax.all_to_all(rows_padded, 'ctx', split_axis=2, concat_axis=1, tiled=True)]
    ppermute x2 -> x0, starting transfers between devices: 5.99 us -> none  [the longest x1 4.71 us: with_halo(): lax.ppermute(tail, axis, [(i, (i + 1) % count) for i in range(ends)])]
  transfers between devices with their start and end apart: 7 -> 0, of which waited for: 5 -> 0; matrix products, arithmetic and copies ran while one was open for 40% -> 0% of each run, Pallas kernels for 0% -> 0%
where the time goes in v1:
time: 74.3 us; the launch traced here: 74 us
  Pallas kernels  67 us (90%)
  local copies, waits for them, and re-layouts  6.34 us (9%)
    pallas_call x1, Pallas kernels, fused_on_device(): pl.pallas_call(fused_kernel, out_shape=jax.ShapeDtypeStruct((1, tok, colu...  67 us
    unnamed x3, local copies, waits for them, and re-layouts  5.06 us

profile of v1, /device:TPU:1, one launch (start us, length us, event | category | flops | bytes accessed | tf_op | source)
XLA Modules:
  0.0 74.0 jit_solution(11860992167951122812)
XLA Ops:
  0.7 1.3 %broadcast_in_dim.3.gate = f32[1,768]{1,0:T(1,128)} reshape(f32[768]{0:T(1024)} %param.18) | data formatting | bytes 6144 | tf_op jit(solution)/shard_map/broadcast_in_dim | solution.py:672
  1.9 1.3 %copy.14.rate = f32[1,12,128]{2,1,0:T(8,128)} copy(f32[1,12,128]{2,0,1:T(1,128)} %param.15) | data formatting | bytes 12288 | tf_op args[2]
  3.2 2.1 %copy.15.second_w = bf16[12,256,64]{2,1,0:T(8,128)(2,1)} copy(bf16[12,256,64]{1,2,0:T(8,128)(2,1)} %param.23) | data formatting | bytes 786432 | tf_op args[10]
  5.4 67.0 %shard_map.127 = bf16[1,128,768]{2,1,0:T(8,128)(2,1)} custom-call(bf16[3,1,128,768]{3,2,1,0:T(8,128)(2,1)} %aqkv.1, bf16[3,1,128,768]{3,2,1,0:T(8,128)(2,1)} %iqkv.1, f32[1,12,128]{2,1,0:T(8,128)} %copy.14.rate, bf16[12,64,256]{2,1,0:T(8,128)(2,1)} %first_w.1, bf16[12,256,64]{2,1,0:T(8,128)(2,1)} %copy.15.second_w, bf16[768,768]{1,0:T(8,128)(2,1)} %out_w.1, ...), custom_call_target="tpu_custom_call" | custom-call | tf_op jit(solution)/shard_map/pallas_call | solution.py:618
  72.4 1.6 %copy.18 = bf16[1,128,768]{2,1,0:T(8,128)(2,1)} copy(bf16[1,128,768]{2,1,0:T(8,128)(2,1)} %shard_map.127) | data formatting | bytes 393216

commit v2 on v1

--- a/solution.py
+++ b/solution.py
@@ -193,6 +193,7 @@
     w2b,
     b1,
     b2,
+    gate_s,
     gain_s,
     shift_s,
     rate_a,
@@ -204,6 +205,7 @@
     parts,
     arrived,
     total,
+    landed,
     load_sem,
     y_send,
     y_recv,
@@ -241,7 +243,7 @@
                 load_sem.at[slab],
             )
         )
-    loads.append(pltpu.make_async_copy(rate.at[0], rates.at[c], load_sem.at[2 * slabs]))
+    loads.append(pltpu.make_async_copy(rate, rates.at[c], load_sem.at[2 * slabs]))
     loads.append(
         pltpu.make_async_copy(
             first_w.at[pl.ds(c * pairs_heads, pairs_heads)], fw, load_sem.at[2 * slabs + 1]
@@ -291,7 +293,7 @@
         )
 
     rate_out = to_partner(
-        rate.at[0], rates.at[c], y_send.at[2 * slabs], y_recv.at[2 * slabs]
+        rate, rates.at[c], y_send.at[2 * slabs], y_recv.at[2 * slabs]
     )
     rate_out.start()
     i_out = [
@@ -312,8 +314,9 @@
         )
         for slab in range(slabs)
     ]
-    for copy in i_out + a_out:
-        copy.start()
+    for first, second in zip(i_out, a_out):
+        first.start()
+        second.start()
 
     seq_ids = lax.broadcasted_iota(jnp.int32, (seq, seq), 1)
     row_ids = lax.broadcasted_iota(jnp.int32, (seq, seq), 0)
@@ -322,15 +325,15 @@
     allowed = (segs == segs.T) & ((seq_ids < len_val) | (seq_ids == row_ids))
     bias[...] = jnp.where(allowed, 0.0, -1e30)
     live = (lax.broadcasted_iota(jnp.int32, (seq, LANE), 0) < len_val).astype(jnp.float32)
-    left_row = lax.broadcasted_iota(jnp.int32, (1, LANE), 1) < HD
     left = lax.broadcasted_iota(jnp.int32, (MB, LANE), 1) < HD
-    left_hidden = lax.broadcasted_iota(jnp.int32, (hidden, LANE), 1) < HD
     left_seq = lax.broadcasted_iota(jnp.int32, (seq, LANE), 1) < HD
     tri = lax.broadcasted_iota(jnp.int32, (MB, MB), 0) >= lax.broadcasted_iota(
         jnp.int32, (MB, MB), 1
     )
     tri = tri.astype(jnp.float32)
     tri_pair = jnp.concatenate([tri, tri], axis=0)
+
+    gate_s[...] = jnp.tanh(gate[...].reshape(1, gate.shape[0]))
 
     for copy in loads:
         copy.wait()
@@ -344,19 +347,13 @@
         shift_s[slab] = pair_row(shift, head)
         b1[slab] = pair_row(first_b, head)
         b2[slab] = pair_row(second_b, head)
-        w1_a = fw[2 * slab]
-        w1_b = fw[2 * slab + 1]
-        w1m[slab, 0:HD] = w1_a.astype(jnp.float32)
-        w1m[slab, HD:LANE] = w1_b.astype(jnp.float32)
-        w1b[slab] = jnp.zeros_like(w1b[slab])
-        w1b[slab, 0:HD, 0:hidden] = w1_a
-        w1b[slab, HD:LANE, hidden : 2 * hidden] = w1_b
-        w2 = jnp.concatenate(
-            [sw[2 * slab].astype(jnp.float32), sw[2 * slab + 1].astype(jnp.float32)], axis=1
-        )
-        w2m[slab] = w2
-        w2b[slab, 0:hidden] = jnp.where(left_hidden, w2, 0.0).astype(jnp.bfloat16)
-        w2b[slab, hidden : 2 * hidden] = jnp.where(left_hidden, 0.0, w2).astype(jnp.bfloat16)
+        for raw, kept, used in ((fw, w1m, w1b), (sw, w2m, w2b)):
+            upper, lower = raw[2 * slab], raw[2 * slab + 1]
+            kept[slab, 0:HD] = upper.astype(jnp.float32)
+            kept[slab, HD:LANE] = lower.astype(jnp.float32)
+            used[slab] = jnp.zeros_like(used[slab])
+            used[slab, 0:HD, 0:hidden] = upper
+            used[slab, HD:LANE, hidden : 2 * hidden] = lower
 
     rate_out.wait_recv()
     for slab in range(slabs):
@@ -364,11 +361,8 @@
         for part in range(seq // tok):
             rows = slice(part * tok, (part + 1) * tok)
             for ahead, store in ((0, rate_a), (1, rate_b)):
-                row = rates[part, pl.ds(head + ahead, 1), :]
+                row = rates[part, head + ahead]
                 store[slab, rows] = jnp.broadcast_to(row, (LANE, tok)).T * live[rows]
-
-    for copy in i_out:
-        copy.wait_recv()
 
     def inner_step(slab, row):
         rows = pl.ds(row, MB)
@@ -385,7 +379,7 @@
         pre = dot_nn(jnp.concatenate([key, query], axis=0), weight_one) + bias_one
         hidden_act, slope = gelu_pair(pre[:MB])
         hidden_b = hidden_act.astype(jnp.bfloat16)
-        normed, inv_std = half_stats(dot_nn(hidden_b, weight_two) + bias_two, left)
+        normed, inv_std = half_stats(dot_nt(hidden_b, weight_two) + bias_two, left)
         scaled = (norm_gain * normed + norm_shift - (value_f - key_f)) * norm_gain
         grad_two = inv_std * (
             scaled - half_mean(scaled, left) - normed * half_mean(scaled * normed, left)
@@ -393,7 +387,7 @@
         e_a = rate_a[slab, rows, :]
         e_b = rate_b[slab, rows, :]
         wide = [e_a] * (hidden // LANE) + [e_b] * (hidden // LANE)
-        grad_one = dot_nt(grad_two.astype(jnp.bfloat16), weight_two) * slope
+        grad_one = dot_nn(grad_two.astype(jnp.bfloat16), weight_two) * slope
         grad_one = grad_one * jnp.concatenate(wide, axis=1)
         grad_two = grad_two * jnp.where(left, e_a, e_b)
         one_b = grad_one.astype(jnp.bfloat16)
@@ -419,34 +413,22 @@
         second_kernel = ((second_kernel + 1.0) * tri_pair).astype(jnp.bfloat16)
         fix_two = dot_nn(second_kernel, two_b)
         fix_two = jnp.where(left, fix_two[:MB], fix_two[MB:])
-        query_out = dot_nn(query_act, weight_two) + bias_two - fix_two
+        query_out = dot_nt(query_act, weight_two) + bias_two - fix_two
         normed_out, _ = half_stats(query_out, left)
         inner[slab, rows, :] = query_f + norm_gain * normed_out + norm_shift
 
-        up_one = dot_tn(key, one_b)
-        one_first = w1m[slab, 0:HD] - up_one[:HD, :hidden]
-        one_second = w1m[slab, HD:LANE] - up_one[HD:, hidden:]
-        up_two = dot_tn(hidden_b, two_b)
-        two_new = w2m[slab] - jnp.where(left_hidden, up_two[:hidden], up_two[hidden:])
-        w1m[slab, 0:HD] = one_first
-        w1m[slab, HD:LANE] = one_second
-        w1b[slab, 0:HD, 0:hidden] = one_first.astype(jnp.bfloat16)
-        w1b[slab, HD:LANE, hidden : 2 * hidden] = one_second.astype(jnp.bfloat16)
-        w2m[slab] = two_new
-        w2b[slab, 0:hidden] = jnp.where(left_hidden, two_new, 0.0).astype(jnp.bfloat16)
-        w2b[slab, hidden : 2 * hidden] = jnp.where(left_hidden, 0.0, two_new).astype(
-            jnp.bfloat16
-        )
+        for kept, used, change in (
+            (w1m, w1b, dot_tn(key, one_b)),
+            (w2m, w2b, dot_tn(two_b, hidden_b)),
+        ):
+            upper = kept[slab, 0:HD] - change[:HD, :hidden]
+            lower = kept[slab, HD:LANE] - change[HD:, hidden:]
+            kept[slab, 0:HD] = upper
+            kept[slab, HD:LANE] = lower
+            used[slab, 0:HD, 0:hidden] = upper.astype(jnp.bfloat16)
+            used[slab, HD:LANE, hidden : 2 * hidden] = lower.astype(jnp.bfloat16)
         b1[slab] = bias_one - jnp.sum(grad_one, axis=0, keepdims=True)
         b2[slab] = bias_two - jnp.sum(grad_two, axis=0, keepdims=True)
-
-    def batch_step(batch, carry):
-        row = pl.multiple_of(batch * MB, MB)
-        for slab in range(slabs):
-            inner_step(slab, row)
-        return carry
-
-    lax.fori_loop(0, seq // MB, batch_step, 0)
 
     def to_video(src, video, spot, step):
         return pltpu.make_async_remote_copy(
@@ -470,6 +452,13 @@
     backs = []
     owns = []
     for slab in range(slabs):
+        i_out[slab].wait_recv()
+
+        def batch_step(batch, carry, slab=slab):
+            inner_step(slab, pl.multiple_of(batch * MB, MB))
+            return carry
+
+        lax.fori_loop(0, seq // MB, batch_step, 0, unroll=True)
         a_loads[slab].wait()
         a_out[slab].wait_recv()
         query, key, value = (a_rows[slab, kind] for kind in range(3))
@@ -482,7 +471,7 @@
             mass = jnp.sum(weights, axis=-1, keepdims=True)
             halves.append(dot_nn(weights.astype(jnp.bfloat16), value) / mass)
         attended = jnp.where(left_seq, halves[0], halves[1])
-        gate_row = jnp.tanh(gate[:, columns(c, slab)])
+        gate_row = gate_s[:, columns(c, slab)]
         comb[slab] = ((attended + gate_row * inner[slab]) * live).astype(jnp.bfloat16)
         spot = c * slabs + slab
         back = to_partner(
@@ -534,52 +523,61 @@
         ],
         axis=0,
     )
-    width = ow.shape[1]
-    chunk = 2 * LANE if width % (2 * LANE) == 0 else width
-    for start in range(0, width, chunk):
-        piece = dot_nn(rows_all, ow[:, start : start + chunk]).astype(jnp.bfloat16)
+    chunks, _, _, chunk = parts.shape
+    r_out = []
+    for at in range(chunks):
+        piece = dot_nn(rows_all, ow[:, at * chunk : (at + 1) * chunk]).astype(jnp.bfloat16)
         for video in range(count):
-            parts[video, :, start : start + chunk] = piece[video * tok : (video + 1) * tok]
-
-    r_out = []
-    for step in range(count - 1, 0, -1):
-        head = lax.rem(h + step, count)
-        copy = pltpu.make_async_remote_copy(
-            src_ref=parts.at[video_of(head)],
-            dst_ref=arrived.at[step - 1],
-            send_sem=r_send.at[step - 1],
-            recv_sem=r_recv.at[step - 1],
-            device_id={"head": head},
-            device_id_type=MESH_ID,
-        )
-        copy.start()
-        r_out.append(copy)
-    for copy in r_out:
-        copy.wait_recv()
-    summed = parts[video_of(h)].astype(jnp.float32)
-    for step in range(count - 1):
-        summed = summed + arrived[step].astype(jnp.float32)
-    total[...] = summed.astype(jnp.bfloat16)
+            parts[at, video] = piece[video * tok : (video + 1) * tok]
+        for step in range(count - 1, 0, -1):
+            head = lax.rem(h + step, count)
+            copy = pltpu.make_async_remote_copy(
+                src_ref=parts.at[at, video_of(head)],
+                dst_ref=arrived.at[at, step - 1],
+                send_sem=r_send.at[at, step - 1],
+                recv_sem=r_recv.at[at, step - 1],
+                device_id={"head": head},
+                device_id_type=MESH_ID,
+            )
+            copy.start()
+            r_out.append(copy)
 
     to_head, to_v = v, video_of(h)
     stays = (to_head == h) & (to_v == v)
-    final = pltpu.make_async_remote_copy(
-        src_ref=total,
-        dst_ref=out.at[0],
-        send_sem=t_send,
-        recv_sem=t_recv,
-        device_id={"head": to_head, "video": to_v},
-        device_id_type=MESH_ID,
-    )
-
-    @pl.when(stays)
-    def _():
-        out[0] = total[...]
+    finals = []
+    for at in range(chunks):
+        for copy in r_out[at * (count - 1) : (at + 1) * (count - 1)]:
+            copy.wait_recv()
+        summed = parts[at, video_of(h)].astype(jnp.float32)
+        for step in range(count - 1):
+            summed = summed + arrived[at, step].astype(jnp.float32)
+        total[at] = summed.astype(jnp.bfloat16)
+        final = pltpu.make_async_remote_copy(
+            src_ref=total.at[at],
+            dst_ref=landed.at[at],
+            send_sem=t_send.at[at],
+            recv_sem=t_recv.at[at],
+            device_id={"head": to_head, "video": to_v},
+            device_id_type=MESH_ID,
+        )
+
+        @pl.when(stays)
+        def _(at=at):
+            landed[at] = total[at]
+
+        @pl.when(jnp.logical_not(stays))
+        def _(final=final):
+            final.start()
+
+        finals.append(final)
 
     @pl.when(jnp.logical_not(stays))
     def _():
-        final.start()
-        final.wait()
+        for final in finals:
+            final.wait()
+
+    for at in range(chunks):
+        out[0, :, at * chunk : (at + 1) * chunk] = landed[at]
 
     for copy in [rate_out] + i_out + a_out + backs + z_out + r_out:
         copy.wait_send()
@@ -609,6 +607,8 @@
     heads = width_dev // HD
     hidden = first_weight.shape[2]
     columns = out_weight.shape[1]
+    chunk = 2 * LANE if columns % (2 * LANE) == 0 else columns
+    chunks = columns // chunk
     half = jnp.bfloat16
     full = jnp.float32
     hbm = pl.BlockSpec(memory_space=pl.ANY)
@@ -623,16 +623,17 @@
         scratch_shapes=[
             pltpu.VMEM((slabs, 3, seq, LANE), half),
             pltpu.VMEM((slabs, 3, seq, LANE), half),
-            pltpu.VMEM((ctx_count, heads, tok), full),
+            pltpu.VMEM((ctx_count, heads, 1, tok), full),
             pltpu.VMEM((2 * slabs,) + first_weight.shape[1:], half),
-            pltpu.VMEM((2 * slabs,) + second_weight.shape[1:], half),
+            pltpu.VMEM((2 * slabs,) + second_weight.shape[:0:-1], half),
             pltpu.VMEM(out_weight.shape, half),
             pltpu.VMEM((slabs, LANE, hidden), full),
             pltpu.VMEM((slabs, LANE, 2 * hidden), half),
-            pltpu.VMEM((slabs, hidden, LANE), full),
-            pltpu.VMEM((slabs, 2 * hidden, LANE), half),
+            pltpu.VMEM((slabs, LANE, hidden), full),
+            pltpu.VMEM((slabs, LANE, 2 * hidden), half),
             pltpu.VMEM((slabs, 1, 2 * hidden), full),
             pltpu.VMEM((slabs, 1, LANE), full),
+            pltpu.VMEM((1, width_dev), full),
             pltpu.VMEM((slabs, 1, LANE), full),
             pltpu.VMEM((slabs, 1, LANE), full),
             pltpu.VMEM((slabs, seq, LANE), full),
@@ -641,9 +642,10 @@
             pltpu.VMEM((slabs, seq, LANE), full),
             pltpu.VMEM((slabs, seq, LANE), half),
             pltpu.VMEM((count, 2 * slabs, tok, LANE), half),
-            pltpu.VMEM((count, tok, columns), half),
-            pltpu.VMEM((count - 1, tok, columns), half),
-            pltpu.VMEM((tok, columns), half),
+            pltpu.VMEM((chunks, count, tok, chunk), half),
+            pltpu.VMEM((chunks, count - 1, tok, chunk), half),
+            pltpu.VMEM((chunks, tok, chunk), half),
+            pltpu.VMEM((chunks, tok, chunk), half),
             dma((2 * slabs + 4,)),
             dma((2 * slabs + 1,)),
             dma((2 * slabs + 1,)),
@@ -652,10 +654,10 @@
             dma((2 * slabs, count - 1)),
             dma((2 * slabs, count - 1)),
             dma((slabs,)),
-            dma((count - 1,)),
-            dma((count - 1,)),
-            dma,
-            dma,
+            dma((chunks, count - 1)),
+            dma((chunks, count - 1)),
+            dma((chunks,)),
+            dma((chunks,)),
         ],
         compiler_params=pltpu.CompilerParams(
             collective_id=0, has_side_effects=True, vmem_limit_bytes=60 * 1024 * 1024
@@ -663,13 +665,13 @@
     )(
         attention_qkv,
         inner_qkv,
-        learn_rate,
+        learn_rate.transpose(1, 0, 2),
         first_weight,
-        second_weight,
+        second_weight.transpose(0, 2, 1),
         out_weight,
         segment_id,
         video_length,
-        gate_alpha[None],
+        gate_alpha,
         inner_gain,
         inner_shift,
         first_bias,

time: 74.3 us -> 56.7 us (0.76)
  the two profiles are of different devices: /device:TPU:1 before, /device:TPU:7 now
where the time goes in v2:
time: 56.7 us; the launch traced here: 56.5 us
  Pallas kernels  54.2 us (96%)
  local copies, waits for them, and re-layouts  1.62 us (3%)
  between operations  0.66 us (1%)
    pallas_call x1, Pallas kernels, fused_on_device(): pl.pallas_call(fused_kernel, out_shape=jax.ShapeDtypeStruct((1, tok, colu...  54.2 us
    unnamed x1, local copies, waits for them, and re-layouts  1.62 us

profile of v2, /device:TPU:7, one launch (start us, length us, event | category | flops | bytes accessed | tf_op | source)
XLA Modules:
  0.0 56.5 jit_solution(551147435486285476)
XLA Ops:
  0.7 54.2 %shard_map.127 = bf16[1,128,768]{2,1,0:T(8,128)(2,1)} custom-call(bf16[3,1,128,768]{3,2,1,0:T(8,128)(2,1)} %aqkv.1, bf16[3,1,128,768]{3,2,1,0:T(8,128)(2,1)} %iqkv.1, f32[12,1,128]{2,1,0:T(1,128)} %bitcast.3, bf16[12,64,256]{2,1,0:T(8,128)(2,1)} %first_w.1, bf16[12,64,256]{2,1,0:T(8,128)(2,1)} %bitcast.2, bf16[768,768]{1,0:T(8,128)(2,1)} %out_w.1, ...), custom_call_target="tpu_custom_call" | custom-call | tf_op jit(solution)/shard_map/pallas_call | solution.py:618
  54.9 1.6 %copy.16 = bf16[1,128,768]{2,1,0:T(8,128)(2,1)} copy(bf16[1,128,768]{2,1,0:T(8,128)(2,1)} %shard_map.127) | data formatting | bytes 393216

commit v3 on v2

--- a/solution.py
+++ b/solution.py
@@ -218,6 +218,8 @@
     r_recv,
     t_send,
     t_recv,
+    low_sem,
+    high_sem,
 ):
     slabs, _, seq, _ = a_rows.shape
     tok = aqkv.shape[2]
@@ -270,17 +272,25 @@
     pl.semaphore_signal(
         barrier, inc=1, device_id={"ctx": other}, device_id_type=MESH_ID
     )
-    everyone = count * count
-    place = h * count + v
-    for step in range(1, everyone):
-        peer = lax.rem(place + step, everyone)
+    below, above = v > 0, v < count - 1
+    for step in range(1, count):
         pl.semaphore_signal(
             barrier,
             inc=1,
-            device_id={"head": peer // count, "video": lax.rem(peer, count)},
+            device_id={"head": lax.rem(h + step, count)},
             device_id_type=MESH_ID,
         )
-    pl.semaphore_wait(barrier, everyone)
+
+    def tell(semaphore, inside, video):
+        @pl.when(inside)
+        def _():
+            pl.semaphore_signal(
+                semaphore, inc=1, device_id={"video": video}, device_id_type=MESH_ID
+            )
+
+    tell(barrier, below, v - 1)
+    tell(barrier, above, v + 1)
+    pl.semaphore_wait(barrier, count + (v + count - 1) // count + (2 * count - 2 - v) // count)
 
     def to_partner(src, dst, send, recv):
         return pltpu.make_async_remote_copy(
@@ -317,6 +327,17 @@
     for first, second in zip(i_out, a_out):
         first.start()
         second.start()
+
+    for semaphore, first, video, last in (
+        (low_sem, below, v + 1, above),
+        (high_sem, above, v - 1, below),
+    ):
+
+        @pl.when(first)
+        def _(semaphore=semaphore):
+            pl.semaphore_wait(semaphore, 1)
+
+        tell(semaphore, last, video)
 
     seq_ids = lax.broadcasted_iota(jnp.int32, (seq, seq), 1)
     row_ids = lax.broadcasted_iota(jnp.int32, (seq, seq), 0)
@@ -505,49 +526,62 @@
     def video_of(head):
         return lax.rem(head, count // 2) * 2 + head // (count // 2)
 
-    for step in range(1, count):
-        source = lax.rem(v + count - step, count)
-        for spot in range(2 * slabs):
-            pltpu.make_async_remote_copy(
-                src_ref=gathered.at[source, spot],
-                dst_ref=gathered.at[source, spot],
-                send_sem=z_send.at[spot, step - 1],
-                recv_sem=z_recv.at[spot, step - 1],
-                device_id={"video": source},
-                device_id_type=MESH_ID,
-            ).wait_recv()
-    rows_all = jnp.concatenate(
-        [
-            jnp.concatenate([gathered[video, spot] for spot in range(2 * slabs)], axis=1)
-            for video in range(count)
-        ],
-        axis=0,
-    )
     chunks, _, _, chunk = parts.shape
-    r_out = []
-    for at in range(chunks):
-        piece = dot_nn(rows_all, ow[:, at * chunk : (at + 1) * chunk]).astype(jnp.bfloat16)
-        for video in range(count):
-            parts[at, video] = piece[video * tok : (video + 1) * tok]
-        for step in range(count - 1, 0, -1):
-            head = lax.rem(h + step, count)
-            copy = pltpu.make_async_remote_copy(
-                src_ref=parts.at[at, video_of(head)],
-                dst_ref=arrived.at[at, step - 1],
-                send_sem=r_send.at[at, step - 1],
-                recv_sem=r_recv.at[at, step - 1],
-                device_id={"head": head},
-                device_id_type=MESH_ID,
-            )
-            copy.start()
-            r_out.append(copy)
+    toward = 1 - 2 * (v // (count // 2))
+
+    def part_copy(video, at):
+        head = owner_of(video)
+        ahead = lax.rem(head - h + count, count)
+        slot = lax.rem(ahead + count - 1, count)
+        return head, pltpu.make_async_remote_copy(
+            src_ref=parts.at[at, video],
+            dst_ref=arrived.at[at, slot],
+            send_sem=r_send.at[at, slot],
+            recv_sem=r_recv.at[at, slot],
+            device_id={"head": head},
+            device_id_type=MESH_ID,
+        )
+
+    videos = []
+    for near in range(count):
+        video = lax.rem(v + toward * near + count, count)
+        videos.append(video)
+        if near:
+            step = lax.rem(v - video + count, count)
+            for spot in range(2 * slabs):
+                pltpu.make_async_remote_copy(
+                    src_ref=gathered.at[video, spot],
+                    dst_ref=gathered.at[video, spot],
+                    send_sem=z_send.at[spot, step - 1],
+                    recv_sem=z_recv.at[spot, step - 1],
+                    device_id={"video": video},
+                    device_id_type=MESH_ID,
+                ).wait_recv()
+        rows_video = jnp.concatenate(
+            [gathered[video, spot] for spot in range(2 * slabs)], axis=1
+        )
+        for at in range(chunks):
+            piece = dot_nn(rows_video, ow[:, at * chunk : (at + 1) * chunk])
+            parts[at, video] = piece.astype(jnp.bfloat16)
+            head, copy = part_copy(video, at)
+
+            @pl.when(head != h)
+            def _(copy=copy):
+                copy.start()
 
     to_head, to_v = v, video_of(h)
     stays = (to_head == h) & (to_v == v)
     finals = []
     for at in range(chunks):
-        for copy in r_out[at * (count - 1) : (at + 1) * (count - 1)]:
-            copy.wait_recv()
+        for step in range(1, count):
+            pltpu.make_async_remote_copy(
+                src_ref=arrived.at[at, step - 1],
+                dst_ref=arrived.at[at, step - 1],
+                send_sem=r_send.at[at, step - 1],
+                recv_sem=r_recv.at[at, step - 1],
+                device_id={"head": lax.rem(h + step, count)},
+                device_id_type=MESH_ID,
+            ).wait_recv()
         summed = parts[at, video_of(h)].astype(jnp.float32)
         for step in range(count - 1):
             summed = summed + arrived[at, step].astype(jnp.float32)
@@ -579,8 +613,15 @@
     for at in range(chunks):
         out[0, :, at * chunk : (at + 1) * chunk] = landed[at]
 
-    for copy in [rate_out] + i_out + a_out + backs + z_out + r_out:
+    for copy in [rate_out] + i_out + a_out + backs + z_out:
         copy.wait_send()
+    for video in videos:
+        for at in range(chunks):
+            head, copy = part_copy(video, at)
+
+            @pl.when(head != h)
+            def _(copy=copy):
+                copy.wait_send()
 
 
 def fused_on_device(
@@ -658,6 +699,8 @@
             dma((chunks, count - 1)),
             dma((chunks,)),
             dma((chunks,)),
+            pltpu.SemaphoreType.REGULAR,
+            pltpu.SemaphoreType.REGULAR,
         ],
         compiler_params=pltpu.CompilerParams(
             collective_id=0, has_side_effects=True, vmem_limit_bytes=60 * 1024 * 1024

time: 56.7 us -> 53.1 us (0.937)
  the two profiles are of different devices: /device:TPU:7 before, /device:TPU:1 now
where the time goes in v3:
time: 53.1 us; the launch traced here: 52.9 us
  Pallas kernels  50.6 us (95%)
  local copies, waits for them, and re-layouts  1.62 us (3%)
  between operations  0.66 us (1%)
    pallas_call x1, Pallas kernels, fused_on_device(): pl.pallas_call(fused_kernel, out_shape=jax.ShapeDtypeStruct((1, tok, colu...  50.6 us
    unnamed x1, local copies, waits for them, and re-layouts  1.62 us

profile of v3, /device:TPU:1, one launch (start us, length us, event | category | flops | bytes accessed | tf_op | source)
XLA Modules:
  0.0 52.9 jit_solution(1754455302568793558)
XLA Ops:
  0.7 50.6 %shard_map.127 = bf16[1,128,768]{2,1,0:T(8,128)(2,1)} custom-call(bf16[3,1,128,768]{3,2,1,0:T(8,128)(2,1)} %aqkv.1, bf16[3,1,128,768]{3,2,1,0:T(8,128)(2,1)} %iqkv.1, f32[12,1,128]{2,1,0:T(1,128)} %bitcast.3, bf16[12,64,256]{2,1,0:T(8,128)(2,1)} %first_w.1, bf16[12,64,256]{2,1,0:T(8,128)(2,1)} %bitcast.2, bf16[768,768]{1,0:T(8,128)(2,1)} %out_w.1, ...), custom_call_target="tpu_custom_call" | custom-call | tf_op jit(solution)/shard_map/pallas_call | solution.py:659
  51.2 1.6 %copy.16 = bf16[1,128,768]{2,1,0:T(8,128)(2,1)} copy(bf16[1,128,768]{2,1,0:T(8,128)(2,1)} %shard_map.127) | data formatting | bytes 393216

commit v4 on v3

--- a/solution.py
+++ b/solution.py
@@ -463,7 +463,7 @@
 
     def spread(src, spot):
         copies = []
-        for step in range(1, count):
+        for step in range(count - 1, 0, -1):
             copy = to_video(src, lax.rem(v + step, count), spot, step)
             copy.start()
             copies.append(copy)

time: 53.1 us -> 52.2 us (0.983)
  Pallas kernels: 50.6 us -> 49.7 us
    pallas_call x1, Pallas kernels: 50.6 us -> 49.7 us  [fused_on_device(): pl.pallas_call(fused_kernel, out_shape=jax.ShapeDtypeStruct((1, tok, colu...]
where the time goes in v4:
time: 52.2 us; the launch traced here: 52 us
  Pallas kernels  49.7 us (95%)
  local copies, waits for them, and re-layouts  1.62 us (3%)
  between operations  0.66 us (1%)
    pallas_call x1, Pallas kernels, fused_on_device(): pl.pallas_call(fused_kernel, out_shape=jax.ShapeDtypeStruct((1, tok, colu...  49.7 us
    unnamed x1, local copies, waits for them, and re-layouts  1.62 us

profile of v4, /device:TPU:1, one launch (start us, length us, event | category | flops | bytes accessed | tf_op | source)
XLA Modules:
  0.0 52.0 jit_solution(2082437222271317724)
XLA Ops:
  0.7 49.7 %shard_map.127 = bf16[1,128,768]{2,1,0:T(8,128)(2,1)} custom-call(bf16[3,1,128,768]{3,2,1,0:T(8,128)(2,1)} %aqkv.1, bf16[3,1,128,768]{3,2,1,0:T(8,128)(2,1)} %iqkv.1, f32[12,1,128]{2,1,0:T(1,128)} %bitcast.3, bf16[12,64,256]{2,1,0:T(8,128)(2,1)} %first_w.1, bf16[12,64,256]{2,1,0:T(8,128)(2,1)} %bitcast.2, bf16[768,768]{1,0:T(8,128)(2,1)} %out_w.1, ...), custom_call_target="tpu_custom_call" | custom-call | tf_op jit(solution)/shard_map/pallas_call | solution.py:659
  50.4 1.6 %copy.16 = bf16[1,128,768]{2,1,0:T(8,128)(2,1)} copy(bf16[1,128,768]{2,1,0:T(8,128)(2,1)} %shard_map.127) | data formatting | bytes 393216
